TPU v7x, 32 devices: a whole 2x2x4 slice. The times are simulated.
32 devices in a mesh: rows: 4 (over y, x), ffn: 8 (over z, core).
Axes of the slice: x: 2, y: 2, z: 4, core: 2. Of those that a mesh axis runs over, the one named last changes fastest.
Arguments:
- tokens: bfloat16 [32768, 1024], P(('rows', 'ffn')), may hold values from -6 to 6
- lengths: int32 [32], P(('rows', 'ffn')), may hold values from 128 to 1024, as said below
- cotangent: bfloat16 [32768, 1024], P(('rows', 'ffn')), may hold values from -6 to 6
- ln_attn_gain: float32 [1024], replicated, may hold values from 0.1 to 1.9
- ln_attn_bias: float32 [1024], replicated, may hold values from -1.75 to 1.75
- w_query: bfloat16 [1024, 1024], P(('rows', 'ffn')), may hold values from -0.1875 to 0.1875
- query_bias: float32 [1024], replicated, may hold values from -3 to 3
- w_key: bfloat16 [1024, 1024], P(('rows', 'ffn')), may hold values from -0.1875 to 0.1875
- w_value: bfloat16 [1024, 1024], P(('rows', 'ffn')), may hold values from -0.1875 to 0.1875
- value_bias: float32 [1024], replicated, may hold values from -3 to 3
- head_scale: float32 [16], replicated, may hold values from 0.3 to 3
- w_out: bfloat16 [1024, 1024], P(('rows', 'ffn')), may hold values from -0.1875 to 0.1875
- out_bias: float32 [1024], replicated, may hold values from -3 to 3
- post_gain: float32 [1024], replicated, may hold values from 0.1 to 1.9
- post_bias: float32 [1024], replicated, may hold values from -1.75 to 1.75
- ffn_gain: float32 [1024], replicated, may hold values from 0.1 to 1.9
- ffn_bias: float32 [1024], replicated, may hold values from -1.75 to 1.75
- w_up: bfloat16 [1024, 4096], P('rows', 'ffn'), may hold values from -1 to 1
- up_bias: float32 [4096], replicated, may hold values from -3 to 3
- mid_gain: float32 [4096], replicated, may hold values from 0.1 to 1.9
- mid_bias: float32 [4096], replicated, may hold values from -1.75 to 1.75
- w_down: bfloat16 [1024, 4096], P('rows', 'ffn'), may hold values from -0.09375 to 0.09375
- down_bias: float32 [1024], replicated, may hold values from -3 to 3
Outputs:
- result: float32 [32768, 1024], P(('rows', 'ffn'))
- grad_tokens: float32 [32768, 1024], P(('rows', 'ffn'))
- grad_ln_attn_gain: float32 [1024], replicated
- grad_ln_attn_bias: float32 [1024], replicated
- grad_w_query: float32 [1024, 1024], P(('rows', 'ffn'))
- grad_query_bias: float32 [1024], replicated
- grad_w_key: float32 [1024, 1024], P(('rows', 'ffn'))
- grad_w_value: float32 [1024, 1024], P(('rows', 'ffn'))
- grad_value_bias: float32 [1024], replicated
- grad_head_scale: float32 [16], replicated
- grad_w_out: float32 [1024, 1024], P(('rows', 'ffn'))
- grad_out_bias: float32 [1024], replicated
- grad_post_gain: float32 [1024], replicated
- grad_post_bias: float32 [1024], replicated
- grad_ffn_gain: float32 [1024], replicated
- grad_ffn_bias: float32 [1024], replicated
- grad_w_up: float32 [1024, 4096], P('rows', 'ffn')
- grad_up_bias: float32 [4096], P('ffn')
- grad_mid_gain: float32 [4096], P('ffn')
- grad_mid_bias: float32 [4096], P('ffn')
- grad_w_down: float32 [1024, 4096], P('rows', 'ffn')
- grad_down_bias: float32 [1024], replicated
Inputs may be any that keep to these rules, and one draw needn't show every extreme that they name: `lengths`: each sequence has between 128 and 1024 valid tokens, at the start of its slots; some sequence has exactly 1024.
All inputs are finite; a program needn't handle non-finite values.
Results may differ from a plain program's by a relative error of at most 0.013.
Values may be sent and summed in bfloat16 or wider, within the bound.
A program may use at most 320 MiB of HBM per device.

v0:
```python
import jax
import jax.numpy as jnp
from jax import lax
from jax.sharding import PartitionSpec as P

epsilon = 1e-05
masked_score = -1e30


def layer_norm(values, gain, shift):
    center = jnp.mean(values, axis=-1, keepdims=True)
    centered = values - center
    spread = jnp.mean(centered * centered, axis=-1, keepdims=True)
    return centered * lax.rsqrt(spread + epsilon) * gain + shift


def exact_gelu(values):
    return jax.nn.gelu(values, approximate=False)


def plain_dot(left, right):
    return jnp.dot(left, right, preferred_element_type=jnp.float32)


def contract_rows(left, right):
    return lax.dot_general(
        left, right, (((0,), (0,)), ((), ())), preferred_element_type=jnp.float32
    )


def contract_cols(left, right):
    return lax.dot_general(
        left, right, (((1,), (1,)), ((), ())), preferred_element_type=jnp.float32
    )


def block_scores(queries, key_rows, first, block_rows, length):
    rows_here = lax.dynamic_slice_in_dim(queries, first, block_rows, 0)
    factor = queries.shape[-1] ** (-0.5)
    scores = (
        jnp.einsum("qhd,khd->hqk", rows_here, key_rows, preferred_element_type=jnp.float32) * factor
    )
    key_pos = jnp.arange(key_rows.shape[0])
    query_pos = first + jnp.arange(block_rows)
    allowed = (key_pos[None, :] <= query_pos[:, None]) & (key_pos[None, :] < length)
    return (rows_here, jnp.where(allowed[None], scores, masked_score))


def attend_forward(queries, key_rows, value_rows, length, block_rows):

    def one_block(first):
        rows_here, scores = block_scores(queries, key_rows, first, block_rows, length)
        peak = jnp.max(scores, axis=-1, keepdims=True)
        weights = jnp.exp(scores - peak)
        totals = jnp.sum(weights, axis=-1, keepdims=True)
        probs = (weights / totals).astype(jnp.bfloat16)
        context = jnp.einsum("hqk,khd->qhd", probs, value_rows, preferred_element_type=jnp.float32)
        return (context, peak[..., 0] + jnp.log(totals[..., 0]))

    firsts = jnp.arange(queries.shape[0] // block_rows) * block_rows
    context, log_totals = lax.map(one_block, firsts)
    return (context.reshape(queries.shape), log_totals)


def attend_backward(queries, key_rows, value_rows, grad_context, log_totals, length, block_rows):
    factor = queries.shape[-1] ** (-0.5)

    def one_block(carry, inputs_here):
        grad_keys, grad_values = carry
        first, block_log = inputs_here
        rows_here, scores = block_scores(queries, key_rows, first, block_rows, length)
        grad_rows = lax.dynamic_slice_in_dim(grad_context, first, block_rows, 0)
        probs = jnp.exp(scores - block_log[..., None])
        grad_probs = jnp.einsum(
            "qhd,khd->hqk", grad_rows, value_rows, preferred_element_type=jnp.float32
        )
        grad_values = grad_values + jnp.einsum(
            "hqk,qhd->khd",
            probs.astype(jnp.bfloat16),
            grad_rows,
            preferred_element_type=jnp.float32,
        )
        inner = jnp.sum(probs * grad_probs, axis=-1, keepdims=True)
        grad_scores = (probs * (grad_probs - inner)).astype(jnp.bfloat16)
        grad_queries = (
            jnp.einsum("hqk,khd->qhd", grad_scores, key_rows, preferred_element_type=jnp.float32)
            * factor
        )
        grad_keys = (
            grad_keys
            + jnp.einsum("hqk,qhd->khd", grad_scores, rows_here, preferred_element_type=jnp.float32)
            * factor
        )
        return ((grad_keys, grad_values), grad_queries)

    firsts = jnp.arange(queries.shape[0] // block_rows) * block_rows
    zeros_like_keys = jnp.zeros(key_rows.shape, jnp.float32)
    (grad_keys, grad_values), grad_queries = lax.scan(
        one_block, (zeros_like_keys, zeros_like_keys), (firsts, log_totals)
    )
    return (grad_queries.reshape(queries.shape), grad_keys, grad_values)


def shards(
    tokens,
    lengths,
    cotangent,
    ln_attn_gain,
    ln_attn_bias,
    w_query,
    query_bias,
    w_key,
    w_value,
    value_bias,
    head_scale,
    w_out,
    out_bias,
    post_gain,
    post_bias,
    ffn_gain,
    ffn_bias,
    w_up,
    up_bias,
    mid_gain,
    mid_bias,
    w_down,
    down_bias,
):
    seq_len, width = tokens.shape
    head_count = head_scale.shape[0]
    head_size = width // head_count
    heads_shape = (seq_len, head_count, head_size)
    block_rows = min(seq_len, 512)
    length = lengths[0]
    valid_rows = (jnp.arange(seq_len) < length)[:, None]
    inputs = tokens.astype(jnp.float32)
    full_query, full_key, full_value, full_out = (
        lax.all_gather(w_query, ("rows", "ffn"), axis=0, tiled=True),
        lax.all_gather(w_key, ("rows", "ffn"), axis=0, tiled=True),
        lax.all_gather(w_value, ("rows", "ffn"), axis=0, tiled=True),
        lax.all_gather(w_out, ("rows", "ffn"), axis=0, tiled=True),
    )
    normed, first_back = jax.vjp(layer_norm, inputs, ln_attn_gain, ln_attn_bias)
    normed_low = normed.astype(jnp.bfloat16)
    queries = (
        (plain_dot(normed_low, full_query) + query_bias).astype(jnp.bfloat16).reshape(heads_shape)
    )
    key_rows = plain_dot(normed_low, full_key).astype(jnp.bfloat16).reshape(heads_shape)
    value_rows = (
        (plain_dot(normed_low, full_value) + value_bias).astype(jnp.bfloat16).reshape(heads_shape)
    )
    context, log_totals = attend_forward(queries, key_rows, value_rows, length, block_rows)
    scaled_low = (context * head_scale[None, :, None]).reshape(seq_len, width).astype(jnp.bfloat16)
    projected = plain_dot(scaled_low, full_out) + out_bias
    branch, second_back = jax.vjp(layer_norm, projected, post_gain, post_bias)
    mixed = inputs + branch
    second, third_back = jax.vjp(layer_norm, mixed, ffn_gain, ffn_bias)
    second_low = second.astype(jnp.bfloat16)
    grad_result = jnp.where(valid_rows, cotangent.astype(jnp.float32), 0.0)
    grad_result_low = grad_result.astype(jnp.bfloat16)
    up_rows, down_rows = (
        lax.all_gather(w_up, "rows", axis=0, tiled=True),
        lax.all_gather(w_down, "rows", axis=0, tiled=True),
    )
    up_full, down_full = (
        lax.all_gather(up_rows, "ffn", axis=1, tiled=True),
        lax.all_gather(down_rows, "ffn", axis=1, tiled=True),
    )
    pre_act = plain_dot(second_low, up_full) + up_bias
    activated, gelu_back = jax.vjp(exact_gelu, pre_act)
    row_mean = jnp.mean(activated, axis=1, keepdims=True)
    inverse = lax.rsqrt(
        jnp.mean(activated * activated, axis=1, keepdims=True) - row_mean * row_mean + epsilon
    )
    unit_rows = (activated - row_mean) * inverse
    mid_low = (unit_rows * mid_gain + mid_bias).astype(jnp.bfloat16)
    ffn_part = contract_cols(mid_low, down_full)
    grad_mid = plain_dot(grad_result_low, down_full)
    grad_down_full = contract_rows(grad_result_low, mid_low)
    scaled_grad = grad_mid * mid_gain
    grad_act = (
        scaled_grad
        - jnp.mean(scaled_grad, axis=1, keepdims=True)
        - unit_rows * jnp.mean(scaled_grad * unit_rows, axis=1, keepdims=True)
    ) * inverse
    grad_pre_low = gelu_back(grad_act)[0].astype(jnp.bfloat16)
    grad_up_full = contract_rows(second_low, grad_pre_low)
    grad_second = contract_cols(grad_pre_low, up_full)
    stacked = jnp.stack(
        [
            jnp.sum(grad_pre_low.astype(jnp.float32), axis=0),
            jnp.sum(grad_mid * unit_rows, axis=0),
            jnp.sum(grad_mid, axis=0),
        ]
    )
    grad_up, grad_down, stacked_own = (
        lax.psum_scatter(grad_up_full, "ffn", scatter_dimension=1, tiled=True),
        lax.psum_scatter(grad_down_full, "ffn", scatter_dimension=1, tiled=True),
        lax.psum_scatter(stacked, "ffn", scatter_dimension=1, tiled=True),
    )
    grad_up, grad_down = (
        lax.psum_scatter(
            grad_up.astype(jnp.bfloat16), "rows", scatter_dimension=0, tiled=True
        ).astype(jnp.float32),
        lax.psum_scatter(
            grad_down.astype(jnp.bfloat16), "rows", scatter_dimension=0, tiled=True
        ).astype(jnp.float32),
    )
    grad_up_bias, grad_mid_gain, grad_mid_bias = lax.psum(
        (stacked_own[0], stacked_own[1], stacked_own[2]), "rows"
    )
    result = jnp.where(valid_rows, mixed + ffn_part + down_bias, 0.0)
    grad_mixed_in, grad_ffn_gain, grad_ffn_bias = third_back(grad_second)
    grad_mixed = grad_result + grad_mixed_in
    grad_projected, grad_post_gain, grad_post_bias = second_back(grad_mixed)
    grad_projected_low = grad_projected.astype(jnp.bfloat16)
    grad_out_weight = contract_rows(scaled_low, grad_projected_low)
    grad_scaled = contract_cols(grad_projected_low, full_out).reshape(heads_shape)
    grad_head_scale = jnp.sum(grad_scaled * context, axis=(0, 2))
    grad_context = (grad_scaled * head_scale[None, :, None]).astype(jnp.bfloat16)
    grad_queries, grad_keys, grad_values = attend_backward(
        queries, key_rows, value_rows, grad_context, log_totals, length, block_rows
    )
    grad_query_low = grad_queries.reshape(seq_len, width).astype(jnp.bfloat16)
    grad_key_low = grad_keys.reshape(seq_len, width).astype(jnp.bfloat16)
    grad_value_low = grad_values.reshape(seq_len, width).astype(jnp.bfloat16)
    grad_query_weight = contract_rows(normed_low, grad_query_low)
    grad_key_weight = contract_rows(normed_low, grad_key_low)
    grad_value_weight = contract_rows(normed_low, grad_value_low)
    grad_normed = (
        contract_cols(grad_query_low, full_query)
        + contract_cols(grad_key_low, full_key)
        + contract_cols(grad_value_low, full_value)
    )
    grad_inputs, grad_ln_gain, grad_ln_bias = first_back(grad_normed)
    grad_tokens = grad_mixed + grad_inputs
    grad_query_weight, grad_key_weight, grad_value_weight, grad_out_weight = (
        lax.psum_scatter(grad_query_weight, ("rows", "ffn"), scatter_dimension=0, tiled=True),
        lax.psum_scatter(grad_key_weight, ("rows", "ffn"), scatter_dimension=0, tiled=True),
        lax.psum_scatter(grad_value_weight, ("rows", "ffn"), scatter_dimension=0, tiled=True),
        lax.psum_scatter(grad_out_weight, ("rows", "ffn"), scatter_dimension=0, tiled=True),
    )
    small_sums = lax.psum(
        (
            grad_ln_gain,
            grad_ln_bias,
            jnp.sum(grad_query_low.astype(jnp.float32), axis=0),
            jnp.sum(grad_value_low.astype(jnp.float32), axis=0),
            grad_head_scale,
            jnp.sum(grad_projected_low.astype(jnp.float32), axis=0),
            grad_post_gain,
            grad_post_bias,
            grad_ffn_gain,
            grad_ffn_bias,
            jnp.sum(grad_result_low.astype(jnp.float32), axis=0),
        ),
        ("rows", "ffn"),
    )
    (
        grad_ln_gain,
        grad_ln_bias,
        grad_query_bias,
        grad_value_bias,
        grad_head_scale,
        grad_out_bias,
        grad_post_gain,
        grad_post_bias,
        grad_ffn_gain,
        grad_ffn_bias,
        grad_down_bias,
    ) = small_sums
    return (
        result,
        grad_tokens,
        grad_ln_gain,
        grad_ln_bias,
        grad_query_weight,
        grad_query_bias,
        grad_key_weight,
        grad_value_weight,
        grad_value_bias,
        grad_head_scale,
        grad_out_weight,
        grad_out_bias,
        grad_post_gain,
        grad_post_bias,
        grad_ffn_gain,
        grad_ffn_bias,
        grad_up,
        grad_up_bias,
        grad_mid_gain,
        grad_mid_bias,
        grad_down,
        grad_down_bias,
    )


def solution(mesh):
    placed = (
        P(("rows", "ffn"), None),
        P(("rows", "ffn")),
        P(("rows", "ffn"), None),
        P(),
        P(),
        P(("rows", "ffn"), None),
        P(),
        P(("rows", "ffn"), None),
        P(("rows", "ffn"), None),
        P(),
        P(),
        P(("rows", "ffn"), None),
        P(),
        P(),
        P(),
        P(),
        P(),
        P("rows", "ffn"),
        P(),
        P(),
        P(),
        P("rows", "ffn"),
        P(),
    )
    return jax.shard_map(
        shards,
        mesh=mesh,
        in_specs=placed,
        out_specs=(
            P(("rows", "ffn"), None),
            P(("rows", "ffn"), None),
            P(),
            P(),
            P(("rows", "ffn"), None),
            P(),
            P(("rows", "ffn"), None),
            P(("rows", "ffn"), None),
            P(),
            P(),
            P(("rows", "ffn"), None),
            P(),
            P(),
            P(),
            P(),
            P(),
            P("rows", "ffn"),
            P("ffn"),
            P("ffn"),
            P("ffn"),
            P("rows", "ffn"),
            P(),
        ),
        check_vma=False,
    )
```

profile of v0, /device:TPU:0, one launch (start us, length us, event | category | flops | bytes accessed | tf_op | source)
XLA Modules:
  0.0 1732.1 jit_solution(4929488624384349497)
XLA Ops:
  11.2 28.0 %all-gather.17.cloned.1.call-done = bf16[1024,512]{1,0:T(8,128)(2,1)} async-done(((bf16[256,512]{1,0:T(8,128)(2,1)}), bf16[1024,512]{1,0:T(8,128)(2,1)}) %all-gather.17.cloned.1.call-update) | async-done | bytes 1048592 | tf_op jit(solution)/shard_map/all_gather | solution.py:162
  49.9 17.8 %all-gather.21.cloned.1.call-done = bf16[1024,512]{1,0:T(8,128)(2,1)} async-done(((bf16[256,512]{1,0:T(8,128)(2,1)}), bf16[1024,512]{1,0:T(8,128)(2,1)}) %all-gather.21.cloned.1.call-update) | async-done | bytes 1048592 | tf_op jit(solution)/shard_map/all_gather | solution.py:163
  67.8 59.4 %all-gather.11.cloned.1.call-done = bf16[1024,1024]{1,0:T(8,128)(2,1)} async-done(((bf16[32,1024]{1,0:T(8,128)(2,1)}), bf16[1024,1024]{1,0:T(8,128)(2,1)}) %all-gather.11.cloned.1.call-update) | async-done | bytes 2097168 | tf_op jit(solution)/shard_map/all_gather | solution.py:139
  132.2 53.3 %all-gather.13.cloned.1.call-done = bf16[1024,1024]{1,0:T(8,128)(2,1)} async-done(((bf16[32,1024]{1,0:T(8,128)(2,1)}), bf16[1024,1024]{1,0:T(8,128)(2,1)}) %all-gather.13.cloned.1.call-update) | async-done | bytes 2097168 | tf_op jit(solution)/shard_map/all_gather | solution.py:140
  191.7 52.0 %all-gather.9.cloned.1.call-done = bf16[1024,1024]{1,0:T(8,128)(2,1)} async-done(((bf16[32,1024]{1,0:T(8,128)(2,1)}), bf16[1024,1024]{1,0:T(8,128)(2,1)}) %all-gather.9.cloned.1.call-update) | async-done | bytes 2097168 | tf_op jit(solution)/shard_map/all_gather | solution.py:138
  249.9 188.3 %while.27 = (s32[]{:T(128)}, f32[2,512,16,64]{1,0,3,2:T(2,128)}, f32[2,16,512]{2,1,0:T(8,128)S(1)}, s32[2]{0:T(128)S(1)}, s32[]{:T(128)}, /*index=5*/bf16[1024,1...) while((s32[]{:T(128)}, f32[2,512,16,64]{1,0,3,2:T(2,128)}, ...), condition=%wide.region_5.6_spmd, body=%wide.region_2.5_spmd.sunk | while | flops 2249188864 | bytes 127146176 | solution.py:61
  305.9 38.2 %dynamic_update_slice.18 = f32[2,512,16,64]{1,0,3,2:T(2,128)} dynamic-update-slice(f32[2,512,16,64]{1,0,3,2:T(2,128)} %get-tuple-element.491, f32[1,512,16,64]{1,0,3,2:T(1,128)} %copy.137, s32[]{:T(128)} %get-tuple-element.490, s32[]{:T(128)} %constant.67.clone.1..sunk, s32[]{:T(128)} %constant.67.clone.1..sunk, s32[]{:T(128)} %constant.67.clone.1..sunk) | dynamic-update-slice | bytes 4194308 | tf_op jit(solution)/shard_map/while/body/jit(dynamic_update_index_in_dim)/dynamic_update_slice | solution.py:61
  399.9 38.2 %dynamic_update_slice.18 = f32[2,512,16,64]{1,0,3,2:T(2,128)} dynamic-update-slice(f32[2,512,16,64]{1,0,3,2:T(2,128)} %get-tuple-element.491, f32[1,512,16,64]{1,0,3,2:T(1,128)} %copy.137, s32[]{:T(128)} %get-tuple-element.490, s32[]{:T(128)} %constant.67.clone.1..sunk, s32[]{:T(128)} %constant.67.clone.1..sunk, s32[]{:T(128)} %constant.67.clone.1..sunk) | dynamic-update-slice | bytes 4194308 | tf_op jit(solution)/shard_map/while/body/jit(dynamic_update_index_in_dim)/dynamic_update_slice | solution.py:61
  458.9 51.2 %fusion.71 = (f32[1024]{0:T(1024)S(1)}, f32[1024]{0:T(1024)S(1)}, f32[1024,4096]{1,0:T(8,128)}, f32[1024,4096]{1,0:T(8,128)}, f32[1024,4096]{1,0:T(8,128)}) fusion(f32[4096]{0:T(1024)S(1)} %copy-done.52, bf16[1024,4096]{1,0:T(8,128)(2,1)} %all-gather.19.cloned.1.call-done, bf16[1024,1024]{0,1:T(8,128)(2,1)} %add_convert_fusion.7.clone.4), kind=kOutput, calls=%fused_computation.145 | convolution fusion | flops 8875145216 | bytes 60841984 | tf_op jit(solution)/shard_map/dot_general | solution.py:22
  510.2 22.7 %multiply_reduce_fusion.1 = (f32[4096]{0:T(1024)S(1)}, f32[1024]{0:T(1024)S(1)}, f32[1024]{0:T(1024)S(1)}, f32[4096]{0:T(1024)S(1)}, f32[1024,4096]{1,0:T(8,128)}) fusion(f32[1024,4096]{1,0:T(8,128)} %get-tuple-element.329, f32[1024]{0:T(1024)S(1)} %get-tuple-element.343, f32[1024]{0:T(1024)S(1)} %get-tuple-element.342, f32[4096]{0:T(1024)S(1)} %copy-done.53, ...), kind=kOutput, calls=%fused_computation.45 | convolution fusion | flops 8630818816 | bytes 44106752 | tf_op jit(solution)/shard_map/dot_general | solution.py:22
  532.9 30.2 %convert_reduce_fusion = (f32[4096]{0:T(1024)S(1)}, bf16[1024,4096]{1,0:T(8,128)(2,1)}, bf16[1024,4096]{1,0:T(8,128)(2,1)}) fusion(f32[1024,4096]{1,0:T(8,128)} %get-tuple-element.330, f32[1024]{0:T(1024)S(1)} %get-tuple-element.353, f32[1024]{0:T(1024)S(1)} %get-tuple-element.343, f32[1024,4096]{1,0:T(8,128)} %get-tuple-element.329, ...), kind=kLoop, calls=%fused_computation.46 | loop fusion | flops 113242112 | bytes 83968000 | tf_op jit(solution)/shard_map/reduce_sum | solution.py:191
  631.4 114.3 %reduce-scatter.20.cloned.1.call-done = f32[1024,512]{1,0:T(8,128)} async-done(((f32[1024,4096]{1,0:T(8,128)}), f32[1024,512]{1,0:T(8,128)}) %reduce-scatter.20.cloned.1.call-update) | async-done | bytes 2097168 | tf_op jit(solution)/shard_map/reduce_scatter | solution.py:197
  761.4 153.2 %reduce-scatter.24.cloned.1.call-done = f32[1024,512]{1,0:T(8,128)} async-done(((f32[1024,4096]{1,0:T(8,128)}), f32[1024,512]{1,0:T(8,128)}) %reduce-scatter.24.cloned.1.call-update) | async-done | bytes 2097168 | tf_op jit(solution)/shard_map/reduce_scatter | solution.py:198
  917.4 229.4 %while.28 = (s32[]{:T(128)}, f32[1024,16,64]{0,2,1:T(8,128)}, f32[1024,16,64]{0,2,1:T(8,128)}, bf16[2,512,16,64]{1,3,2,0:T(8,128)(2,1)}, s32[2]{0:T(128)S(1)}, /...) while((s32[]{:T(128)}, f32[1024,16,64]{0,2,1:T(8,128)}, ...), condition=%wide.region_20.21_spmd.clone, body=%wide.region_18.20_spmd.clone.sunk | while | flops 5501347328 | bytes 375626592 | solution.py:98
  939.4 25.7 %multiply_reduce_fusion.13 = (f32[16,512]{1,0:T(8,128)S(1)}, f32[16,512,1024]{2,1,0:T(8,128)}) fusion(f32[16,512,1024]{2,1,0:T(8,128)} %fusion.145, f32[16,512]{1,0:T(8,128)S(1)} %dynamic-slice_bitcast_fusion.2, pred[512,1024]{1,0:T(8,128)(4,1)S(1)} %fusion.146, bf16[1024,16,64]{0,2,1:T(8,128)(2,1)S(1)} %copy-done.8, ...), kind=kOutput, calls=%fused_computation.18.clone.1 | convolution fusion | flops 1115676672 | bytes 70844416 | tf_op jit(solution)/shard_map/while/body/eval_jaxpr/qhd,khd->hqk/dot_general | solution.py:74
  965.2 28.2 %multiply_convert_fusion.6 = bf16[16,512,1024]{2,1,0:T(8,128)(2,1)} fusion(f32[16,512,1024]{2,1,0:T(8,128)} %get-tuple-element.477, f32[16,512,1024]{2,1,0:T(8,128)} %fusion.145, f32[16,512]{1,0:T(8,128)S(1)} %get-tuple-element.478, f32[16,512]{1,0:T(8,128)S(1)} %dynamic-slice_bitcast_fusion.2, pred[512,1024]{1,0:T(8,128)(4,1)S(1)} %fusion.146), kind=kLoop, calls=%fused_computation.17.clone.1 | loop fusion | flops 50331648 | bytes 84475904 | tf_op jit(solution)/shard_map/while/body/eval_jaxpr/convert_element_type | solution.py:84
  1013.8 18.0 %bitcast_add_fusion.5 = f32[1024,16,64]{0,2,1:T(8,128)} fusion(f32[1024,16,64]{0,2,1:T(8,128)} %get-tuple-element.528, f32[16,512,1024]{2,1,0:T(8,128)} %fusion.145, f32[16,512]{1,0:T(8,128)S(1)} %dynamic-slice_bitcast_fusion.2, pred[512,1024]{1,0:T(8,128)(4,1)S(1)} %fusion.146, pred[]{:T(512)S(6)} %compare.3, ...), kind=kOutput, calls=%fused_computation.23.clone.1 | convolution fusion | flops 1109393408 | bytes 43548676 | tf_op jit(solution)/shard_map/while/body/eval_jaxpr/hqk,qhd->khd/dot_general | solution.py:77
  1053.2 25.6 %multiply_reduce_fusion.13 = (f32[16,512]{1,0:T(8,128)S(1)}, f32[16,512,1024]{2,1,0:T(8,128)}) fusion(f32[16,512,1024]{2,1,0:T(8,128)} %fusion.145, f32[16,512]{1,0:T(8,128)S(1)} %dynamic-slice_bitcast_fusion.2, pred[512,1024]{1,0:T(8,128)(4,1)S(1)} %fusion.146, bf16[1024,16,64]{0,2,1:T(8,128)(2,1)S(1)} %copy-done.8, ...), kind=kOutput, calls=%fused_computation.18.clone.1 | convolution fusion | flops 1115676672 | bytes 70844416 | tf_op jit(solution)/shard_map/while/body/eval_jaxpr/qhd,khd->hqk/dot_general | solution.py:74
  1078.8 27.8 %multiply_convert_fusion.6 = bf16[16,512,1024]{2,1,0:T(8,128)(2,1)} fusion(f32[16,512,1024]{2,1,0:T(8,128)} %get-tuple-element.477, f32[16,512,1024]{2,1,0:T(8,128)} %fusion.145, f32[16,512]{1,0:T(8,128)S(1)} %get-tuple-element.478, f32[16,512]{1,0:T(8,128)S(1)} %dynamic-slice_bitcast_fusion.2, pred[512,1024]{1,0:T(8,128)(4,1)S(1)} %fusion.146), kind=kLoop, calls=%fused_computation.17.clone.1 | loop fusion | flops 50331648 | bytes 84475904 | tf_op jit(solution)/shard_map/while/body/eval_jaxpr/convert_element_type | solution.py:84
  1127.5 19.1 %bitcast_add_fusion.5 = f32[1024,16,64]{0,2,1:T(8,128)} fusion(f32[1024,16,64]{0,2,1:T(8,128)} %get-tuple-element.528, f32[16,512,1024]{2,1,0:T(8,128)} %fusion.145, f32[16,512]{1,0:T(8,128)S(1)} %dynamic-slice_bitcast_fusion.2, pred[512,1024]{1,0:T(8,128)(4,1)S(1)} %fusion.146, pred[]{:T(512)S(6)} %compare.3, ...), kind=kOutput, calls=%fused_computation.23.clone.1 | convolution fusion | flops 1109393408 | bytes 43548676 | tf_op jit(solution)/shard_map/while/body/eval_jaxpr/hqk,qhd->khd/dot_general | solution.py:77
  1226.5 39.9 %all-reduce = (f32[1024]{0:T(1024)}, f32[1024]{0:T(1024)}, f32[1024]{0:T(1024)}, f32[1024]{0:T(1024)}, f32[16]{0:T(128)}, /*index=5*/f32[1024]{0:T(1024)}, f32[1...) all-reduce(f32[1024]{0:T(1024)S(1)} %get-tuple-element.263, ...), channel_id=1, replica_groups=mesh['rows'=4,'ffn'=8] {'rows','ffn'}, use_global_device_ids=true, to_apply=%region_24.25 | all-reduce | flops 10256 | bytes 82048 | tf_op jit(solution)/shard_map/psum | solution.py:243
  1298.4 142.7 %reduce-scatter.16.cloned.1.call-done = f32[32,1024]{1,0:T(8,128)} async-done(((f32[1024,1024]{1,0:T(8,128)}), f32[32,1024]{1,0:T(8,128)}) %reduce-scatter.16.cloned.1.call-update) | async-done | bytes 131088 | tf_op jit(solution)/shard_map/reduce_scatter | solution.py:240
  1441.1 142.3 %reduce-scatter.14.cloned.1.call-done = f32[32,1024]{1,0:T(8,128)} async-done(((f32[1024,1024]{1,0:T(8,128)}), f32[32,1024]{1,0:T(8,128)}) %reduce-scatter.14.cloned.1.call-update) | async-done | bytes 131088 | tf_op jit(solution)/shard_map/reduce_scatter | solution.py:239
  1583.3 141.9 %reduce-scatter.18.cloned.1.call-done = f32[32,1024]{1,0:T(8,128)} async-done(((f32[1024,1024]{1,0:T(8,128)}), f32[32,1024]{1,0:T(8,128)}) %reduce-scatter.18.cloned.1.call-update) | async-done | bytes 131088 | tf_op jit(solution)/shard_map/reduce_scatter | solution.py:241
  (328 shorter events, 437.2 us)
Async XLA Ops:
  7.2 32.0 %all-gather.17.cloned.1.call-start = ((), (), s32[]{:S(2)}) async-start(), calls=%async_computation.13 | async-start | bytes 1310720 | tf_op jit(solution)/shard_map/all_gather | solution.py:162
  7.9 59.8 %all-gather.21.cloned.1.call-start = ((), (), s32[]{:S(2)}) async-start(), calls=%async_computation.15 | async-start | bytes 1310720 | tf_op jit(solution)/shard_map/all_gather | solution.py:163
  8.7 118.6 %all-gather.11.cloned.1.call-start = ((), (), s32[]{:S(2)}) async-start(), calls=%async_computation.10 | async-start | bytes 2162688 | tf_op jit(solution)/shard_map/all_gather | solution.py:139
  9.4 176.0 %all-gather.13.cloned.1.call-start = ((), (), s32[]{:S(2)}) async-start(), calls=%async_computation.11 | async-start | bytes 2162688 | tf_op jit(solution)/shard_map/all_gather | solution.py:140
  10.0 233.6 %all-gather.9.cloned.1.call-start = ((), (), s32[]{:S(2)}) async-start(), calls=%async_computation.9 | async-start | bytes 2162688 | tf_op jit(solution)/shard_map/all_gather | solution.py:138
  10.6 433.8 %all-gather.15.cloned.1.call-start = ((), (), s32[]{:S(2)}) async-start(), calls=%async_computation.12 | async-start | bytes 2162688 | tf_op jit(solution)/shard_map/all_gather | solution.py:141
  11.2 447.7 %all-gather.19.cloned.1.call-start = ((), (), s32[]{:S(2)}) async-start(), calls=%async_computation.14 | async-start | bytes 9437184 | tf_op jit(solution)/shard_map/all_gather | solution.py:166
  39.3 470.8 %all-gather.23.cloned.1.call-start = ((), (), s32[]{:S(2)}) async-start(), calls=%async_computation.16 | async-start | bytes 9437184 | tf_op jit(solution)/shard_map/all_gather | solution.py:167
  48.7 195.0 %copy-start.37 = (f32[1024]{0:T(1024)}, f32[1024]{0:T(1024)S(1)}, u32[]{:S(2)}) copy-start(f32[1024]{0:T(1024)S(1)} %broadcast_multiply_fusion.5) | copy-start | bytes 12292
  49.9 193.8 %copy-start.43 = (f32[1024]{0:T(1024)}, f32[1024]{0:T(1024)S(1)}, u32[]{:S(2)}) copy-start(f32[1024]{0:T(1024)S(1)} %fusion.52) | copy-start | bytes 12292
  67.8 117.7 %copy-start.75 = (f32[1024]{0:T(1024)S(1)}, f32[1024]{0:T(1024)}, u32[]{:S(2)}) copy-start(f32[1024]{0:T(1024)} %param.36) | copy-start | bytes 12292
  67.8 677.9 %reduce-scatter.20.cloned.1.call-start = ((), (), s32[]{:S(2)}) async-start(), calls=%async_computation.21 | async-start | bytes 18874368 | tf_op jit(solution)/shard_map/reduce_scatter | solution.py:197
  132.2 111.5 %copy-start.76 = (f32[1024]{0:T(1024)S(1)}, f32[1024]{0:T(1024)}, u32[]{:S(2)}) copy-start(f32[1024]{0:T(1024)} %param.33) | copy-start | bytes 12292
  578.6 336.0 %reduce-scatter.24.cloned.1.call-start = ((), (), s32[]{:S(2)}) async-start(), calls=%async_computation.23 | async-start | bytes 18874368 | tf_op jit(solution)/shard_map/reduce_scatter | solution.py:198
  593.0 673.3 %reduce-scatter.28.cloned.1.call-start = ((), (), s32[]{:S(2)}) async-start(), calls=%async_computation.25 | async-start | bytes 2359296
  631.3 647.4 %reduce-scatter.22.cloned.1.call-start = ((), (), s32[]{:S(2)}) async-start(), calls=%async_computation.22 | async-start | bytes 1310720 | tf_op jit(solution)/shard_map/reduce_scatter | solution.py:202
  748.4 532.1 %reduce-scatter.26.cloned.1.call-start = ((), (), s32[]{:S(2)}) async-start(), calls=%async_computation.24 | async-start | bytes 1310720 | tf_op jit(solution)/shard_map/reduce_scatter | solution.py:205
  759.4 158.0 %copy-start.2 = (bf16[1024,16,64]{0,2,1:T(8,128)(2,1)S(1)}, bf16[1024,16,64]{0,2,1:T(8,128)(2,1)}, u32[]{:S(2)}) copy-start(bf16[1024,16,64]{0,2,1:T(8,128)(2,1)} %copy-done.1) | copy-start | bytes 6291460
  759.4 158.0 %copy-start.26 = (f32[2,16,512]{2,1,0:T(8,128)S(1)}, f32[2,16,512]{2,1,0:T(8,128)}, u32[]{:S(2)}) copy-start(f32[2,16,512]{2,1,0:T(8,128)} %copy-done.25) | copy-start | bytes 196612
  759.4 158.0 %copy-start.81 = (s32[2]{0:T(128)S(1)}, s32[2]{0:T(128)}, u32[]{:S(2)}) copy-start(s32[2]{0:T(128)} %copy-done.80) | copy-start | bytes 28
  917.3 381.1 %reduce-scatter.12.cloned.1.call-start = ((), (), s32[]{:S(2)}) async-start(), calls=%async_computation.17 | async-start | bytes 4325376 | tf_op jit(solution)/shard_map/reduce_scatter | solution.py:238
  1157.2 283.9 %reduce-scatter.16.cloned.1.call-start = ((), (), s32[]{:S(2)}) async-start(), calls=%async_computation.19 | async-start | bytes 4325376 | tf_op jit(solution)/shard_map/reduce_scatter | solution.py:240
  1165.5 417.8 %reduce-scatter.14.cloned.1.call-start = ((), (), s32[]{:S(2)}) async-start(), calls=%async_computation.18 | async-start | bytes 4325376 | tf_op jit(solution)/shard_map/reduce_scatter | solution.py:239
  1173.8 551.4 %reduce-scatter.18.cloned.1.call-start = ((), (), s32[]{:S(2)}) async-start(), calls=%async_computation.20 | async-start | bytes 4325376 | tf_op jit(solution)/shard_map/reduce_scatter | solution.py:241
  (80 other events, 926.1 us)
Sparse Core Ops, SparseCore 0:
  9.9 29.3 all-gather.16
  41.1 26.6 all-gather.20
  70.7 56.4 all-gather.10
  130.1 55.3 all-gather.12
  188.3 55.3 all-gather.8
  246.5 55.3 all-gather.14
  303.5 81.0 all-gather.18
  386.2 80.4 all-gather.22
  578.7 166.9 reduce-scatter.19
  747.9 166.6 reduce-scatter.23
  916.8 34.1 reduce-scatter.27
  953.8 26.1 reduce-scatter.21
  983.1 27.7 reduce-scatter.25
  1157.3 141.0 reduce-scatter.11
  1301.1 139.9 reduce-scatter.15
  1443.8 139.5 reduce-scatter.13
  1586.0 139.1 reduce-scatter.17
where the time goes:
time: 1750 us; the launch traced here: 1730 us
  waiting for transfers between devices  925 us (53%)
  matrix products  420 us (24%)
  other arithmetic  171 us (10%)
  local copies, waits for them, and re-layouts  140 us (8%)
  blocking collectives  50.5 us (3%)
    reduce_scatter x1, waiting for transfers between devices, shards(): lax.psum_scatter(grad_down_full, 'ffn', scatter_dimension=1, tiled=True)  153 us
    reduce_scatter x1, waiting for transfers between devices, shards(): lax.psum_scatter(grad_value_weight, ('rows', 'ffn'), scatter_dimension=0,...  143 us
    reduce_scatter x1, waiting for transfers between devices, shards(): lax.psum_scatter(grad_key_weight, ('rows', 'ffn'), scatter_dimension=0, t...  142 us
    reduce_scatter x1, waiting for transfers between devices, shards(): lax.psum_scatter(grad_out_weight, ('rows', 'ffn'), scatter_dimension=0, t...  142 us
    reduce_scatter x1, waiting for transfers between devices, shards(): lax.psum_scatter(grad_up_full, 'ffn', scatter_dimension=1, tiled=True)  114 us
    dot_general x6, matrix products, plain_dot(): return jnp.dot(left, right, preferred_element_type=jnp.float32)  96.6 us
    dynamic_update_slice x4, local copies, waits for them, and re-layouts, attend_forward(): context, log_totals = lax.map(one_block, firsts)  83.4 us
    dot_general x4, matrix products, block_scores(): jnp.einsum('qhd,khd->hqk', rows_here, key_rows, preferred_element_type=jn...  67 us
  transfers between devices with their start and end apart: 17, of which 11 were waited for; matrix products, arithmetic and copies ran while one was open for 37% of the time, Pallas kernels for 0%

commit v1 on v0

--- a/solution.py
+++ b/solution.py
@@ -5,6 +5,18 @@
 
 epsilon = 1e-05
 masked_score = -1e30
+
+
+def doubled_up(array, axis, dim):
+    ways, here, step = (lax.axis_size(axis), lax.axis_index(axis), array.shape[dim])
+    line, have = (array, 1)
+    while have < ways:
+        line = jnp.concatenate(
+            [line, lax.ppermute(line, axis, [(d, (d - have) % ways) for d in range(ways)])],
+            axis=dim,
+        )
+        have = 2 * have
+    return jnp.roll(line, here * step, axis=dim)
 
 
 def layer_norm(values, gain, shift):
@@ -136,7 +148,7 @@
     inputs = tokens.astype(jnp.float32)
     full_query, full_key, full_value, full_out = (
         lax.all_gather(w_query, ("rows", "ffn"), axis=0, tiled=True),
-        lax.all_gather(w_key, ("rows", "ffn"), axis=0, tiled=True),
+        doubled_up(w_key, ("rows", "ffn"), 0),
         lax.all_gather(w_value, ("rows", "ffn"), axis=0, tiled=True),
         lax.all_gather(w_out, ("rows", "ffn"), axis=0, tiled=True),
     )

time: 1750 us -> 1570 us (0.90)
  waiting for transfers between devices: 925 us -> 720 us
    reduce_scatter x1, waiting for transfers between devices: 142 us -> 0.01 us  [shards(): lax.psum_scatter(grad_out_weight, ('rows', 'ffn'), scatter_dimension=0, t...]
    all_gather x1 -> x0, waiting for transfers between devices: 59.4 us -> none  [shards(): lax.all_gather(w_key, ('rows', 'ffn'), axis=0, tiled=True)]
    ppermute x0 -> x5, waiting for transfers between devices: none -> 43.5 us  [doubled_up(): lax.ppermute(line, axis, [(d, (d - have) % ways) for d in range(ways)])]
    all_gather x1, waiting for transfers between devices: 53.3 us -> 11.4 us  [shards(): lax.all_gather(w_value, ('rows', 'ffn'), axis=0, tiled=True)]
    all_gather x1, waiting for transfers between devices: 17.8 us -> 0.02 us  [shards(): lax.all_gather(w_down, 'rows', axis=0, tiled=True)]
    unnamed x164 -> x176, local copies, waits for them, and re-layouts: 40.8 us -> 52.9 us
  transfers between devices with their start and end apart: 17 -> 21, of which waited for: 11 -> 13; matrix products, arithmetic and copies ran while one was open for 37% -> 43% of each run, Pallas kernels for 0% -> 0%
where the time goes in v1:
time: 1570 us; the launch traced here: 1550 us
  waiting for transfers between devices  720 us (46%)
  matrix products  417 us (27%)
  other arithmetic  180 us (11%)
  local copies, waits for them, and re-layouts  154 us (10%)
  blocking collectives  50.5 us (3%)
  between operations  15.9 us (1%)
    reduce_scatter x1, waiting for transfers between devices, shards(): lax.psum_scatter(grad_down_full, 'ffn', scatter_dimension=1, tiled=True)  148 us
    reduce_scatter x1, waiting for transfers between devices, shards(): lax.psum_scatter(grad_value_weight, ('rows', 'ffn'), scatter_dimension=0,...  142 us
    reduce_scatter x1, waiting for transfers between devices, shards(): lax.psum_scatter(grad_key_weight, ('rows', 'ffn'), scatter_dimension=0, t...  142 us
    reduce_scatter x1, waiting for transfers between devices, shards(): lax.psum_scatter(grad_up_full, 'ffn', scatter_dimension=1, tiled=True)  125 us
    dot_general x6, matrix products, plain_dot(): return jnp.dot(left, right, preferred_element_type=jnp.float32)  96.3 us
    dynamic_update_slice x4, local copies, waits for them, and re-layouts, attend_forward(): context, log_totals = lax.map(one_block, firsts)  83.4 us
    dot_general x4, matrix products, block_scores(): jnp.einsum('qhd,khd->hqk', rows_here, key_rows, preferred_element_type=jn...  66.9 us
    convert_element_type x2, other arithmetic, one_block(): grad_scores = (probs * (grad_probs - inner)).astype(jnp.bfloat16)  56.5 us
  transfers between devices with their start and end apart: 21, of which 13 were waited for; matrix products, arithmetic and copies ran while one was open for 43% of the time, Pallas kernels for 0%

profile of v1, /device:TPU:0, one launch (start us, length us, event | category | flops | bytes accessed | tf_op | source)
XLA Modules:
  0.0 1554.6 jit_solution(10046734970111701029)
XLA Ops:
  10.6 28.6 %all-gather.14.cloned.1.call-done = bf16[1024,512]{1,0:T(8,128)(2,1)} async-done(((bf16[256,512]{1,0:T(8,128)(2,1)}), bf16[1024,512]{1,0:T(8,128)(2,1)}) %all-gather.14.cloned.1.call-update) | async-done | bytes 1048592 | tf_op jit(solution)/shard_map/all_gather | solution.py:174
  139.6 51.9 %all-gather.8.cloned.1.call-done = bf16[1024,1024]{1,0:T(8,128)(2,1)} async-done(((bf16[32,1024]{1,0:T(8,128)(2,1)}), bf16[1024,1024]{1,0:T(8,128)(2,1)}) %all-gather.8.cloned.1.call-update) | async-done | bytes 2097168 | tf_op jit(solution)/shard_map/all_gather | solution.py:150
  197.9 189.6 %while.27 = (s32[]{:T(128)}, f32[2,512,16,64]{1,0,3,2:T(2,128)}, f32[2,16,512]{2,1,0:T(8,128)}, s32[2]{0:T(128)S(1)}, s32[]{:T(128)}, /*index=5*/bf16[1024,16,64...) while((s32[]{:T(128)}, f32[2,512,16,64]{1,0,3,2:T(2,128)}, ...), condition=%wide.region_5.6_spmd, body=%wide.region_2.5_spmd.sunk | while | flops 2249188864 | bytes 127146688 | solution.py:73
  254.2 38.2 %dynamic_update_slice.18 = f32[2,512,16,64]{1,0,3,2:T(2,128)} dynamic-update-slice(f32[2,512,16,64]{1,0,3,2:T(2,128)} %get-tuple-element.501, f32[1,512,16,64]{1,0,3,2:T(1,128)} %copy.137, s32[]{:T(128)} %get-tuple-element.500, s32[]{:T(128)} %constant.74.clone.1..sunk, s32[]{:T(128)} %constant.74.clone.1..sunk, s32[]{:T(128)} %constant.74.clone.1..sunk) | dynamic-update-slice | bytes 4194308 | tf_op jit(solution)/shard_map/while/body/jit(dynamic_update_index_in_dim)/dynamic_update_slice | solution.py:73
  328.8 16.8 %fusion.137 = f32[1,512,16,64]{1,3,2,0:T(8,128)S(1)} fusion(bf16[1024,16,64]{0,2,1:T(8,128)(2,1)S(1)} %copy-done.7, f32[16,512,1024]{2,1,0:T(8,128)} %get-tuple-element.474, f32[16,512]{1,0:T(8,128)S(1)} %fusion.136, f32[16,512]{1,0:T(8,128)S(1)} %get-tuple-element.475, pred[512,1024]{1,0:T(8,128)(4,1)S(1)} %fusion.134), kind=kOutput, calls=%fused_computation.8.clone.1 | convolution fusion | flops 1115684864 | bytes 38338560 | tf_op jit(solution)/shard_map/while/body/eval_jaxpr/hqk,khd->qhd/dot_general | solution.py:69
  349.1 38.2 %dynamic_update_slice.18 = f32[2,512,16,64]{1,0,3,2:T(2,128)} dynamic-update-slice(f32[2,512,16,64]{1,0,3,2:T(2,128)} %get-tuple-element.501, f32[1,512,16,64]{1,0,3,2:T(1,128)} %copy.137, s32[]{:T(128)} %get-tuple-element.500, s32[]{:T(128)} %constant.74.clone.1..sunk, s32[]{:T(128)} %constant.74.clone.1..sunk, s32[]{:T(128)} %constant.74.clone.1..sunk) | dynamic-update-slice | bytes 4194308 | tf_op jit(solution)/shard_map/while/body/jit(dynamic_update_index_in_dim)/dynamic_update_slice | solution.py:73
  408.0 51.2 %fusion.75 = (f32[1024]{0:T(1024)S(1)}, f32[1024]{0:T(1024)S(1)}, f32[1024,4096]{1,0:T(8,128)}, f32[1024,4096]{1,0:T(8,128)}, f32[1024,4096]{1,0:T(8,128)}) fusion(f32[4096]{0:T(1024)S(1)} %copy-done.53, bf16[1024,4096]{1,0:T(8,128)(2,1)} %all-gather.16.cloned.1.call-done, bf16[1024,1024]{0,1:T(8,128)(2,1)} %add_convert_fusion.7.clone.4), kind=kOutput, calls=%fused_computation.169 | convolution fusion | flops 8875145216 | bytes 60841984 | tf_op jit(solution)/shard_map/dot_general | solution.py:34
  459.3 22.6 %multiply_reduce_fusion.1 = (f32[4096]{0:T(1024)S(1)}, f32[1024]{0:T(1024)S(1)}, f32[1024]{0:T(1024)S(1)}, f32[4096]{0:T(1024)S(1)}, f32[1024,4096]{1,0:T(8,128)}) fusion(f32[1024,4096]{1,0:T(8,128)} %get-tuple-element.329, f32[1024]{0:T(1024)S(1)} %get-tuple-element.353, f32[1024]{0:T(1024)S(1)} %get-tuple-element.352, f32[4096]{0:T(1024)S(1)} %copy-done.54, ...), kind=kOutput, calls=%fused_computation.45 | convolution fusion | flops 8630818816 | bytes 44106752 | tf_op jit(solution)/shard_map/dot_general | solution.py:34
  482.0 30.2 %convert_reduce_fusion = (f32[4096]{0:T(1024)S(1)}, bf16[1024,4096]{1,0:T(8,128)(2,1)}, bf16[1024,4096]{1,0:T(8,128)(2,1)}) fusion(f32[1024,4096]{1,0:T(8,128)} %get-tuple-element.330, f32[1024]{0:T(1024)S(1)} %get-tuple-element.363, f32[1024]{0:T(1024)S(1)} %get-tuple-element.353, f32[1024,4096]{1,0:T(8,128)} %get-tuple-element.329, ...), kind=kLoop, calls=%fused_computation.46 | loop fusion | flops 113242112 | bytes 83968000 | tf_op jit(solution)/shard_map/reduce_sum | solution.py:203
  569.7 125.2 %reduce-scatter.20.cloned.1.call-done = f32[1024,512]{1,0:T(8,128)} async-done(((f32[1024,4096]{1,0:T(8,128)}), f32[1024,512]{1,0:T(8,128)}) %reduce-scatter.20.cloned.1.call-update) | async-done | bytes 2097168 | tf_op jit(solution)/shard_map/reduce_scatter | solution.py:209
  715.7 148.2 %reduce-scatter.24.cloned.1.call-done = f32[1024,512]{1,0:T(8,128)} async-done(((f32[1024,4096]{1,0:T(8,128)}), f32[1024,512]{1,0:T(8,128)}) %reduce-scatter.24.cloned.1.call-update) | async-done | bytes 2097168 | tf_op jit(solution)/shard_map/reduce_scatter | solution.py:210
  881.8 230.1 %while.28 = (s32[]{:T(128)}, f32[1024,16,64]{0,2,1:T(8,128)}, f32[1024,16,64]{0,2,1:T(8,128)}, bf16[2,512,16,64]{1,3,2,0:T(8,128)(2,1)}, s32[2]{0:T(128)S(1)}, /...) while((s32[]{:T(128)}, f32[1024,16,64]{0,2,1:T(8,128)}, ...), condition=%wide.region_20.21_spmd.clone, body=%wide.region_18.20_spmd.clone.sunk | while | flops 5501347328 | bytes 375626592 | solution.py:110
  884.7 17.2 %fusion.147 = f32[16,512,1024]{2,1,0:T(8,128)} fusion(bf16[1024,16,64]{0,2,1:T(8,128)(2,1)S(1)} %get-tuple-element.557, bf16[1024,16,64]{0,2,1:T(8,128)(2,1)} %get-tuple-element.555, s32[]{:T(128)S(6)} %select_n.90), kind=kOutput, calls=%fused_computation.32.clone.1 | convolution fusion | flops 1073741824 | bytes 36700164 | tf_op jit(solution)/shard_map/while/body/eval_jaxpr/qhd,khd->hqk/dot_general | solution.py:53
  903.7 25.8 %multiply_reduce_fusion.13 = (f32[16,512]{1,0:T(8,128)S(1)}, f32[16,512,1024]{2,1,0:T(8,128)}) fusion(f32[16,512,1024]{2,1,0:T(8,128)} %fusion.147, f32[16,512]{1,0:T(8,128)S(1)} %dynamic-slice_bitcast_fusion.2, pred[512,1024]{1,0:T(8,128)(4,1)S(1)} %fusion.148, bf16[1024,16,64]{0,2,1:T(8,128)(2,1)S(1)} %copy-done.8, ...), kind=kOutput, calls=%fused_computation.18.clone.1 | convolution fusion | flops 1115676672 | bytes 70844416 | tf_op jit(solution)/shard_map/while/body/eval_jaxpr/qhd,khd->hqk/dot_general | solution.py:86
  929.5 28.3 %multiply_convert_fusion.6 = bf16[16,512,1024]{2,1,0:T(8,128)(2,1)} fusion(f32[16,512,1024]{2,1,0:T(8,128)} %get-tuple-element.487, f32[16,512,1024]{2,1,0:T(8,128)} %fusion.147, f32[16,512]{1,0:T(8,128)S(1)} %get-tuple-element.488, f32[16,512]{1,0:T(8,128)S(1)} %dynamic-slice_bitcast_fusion.2, pred[512,1024]{1,0:T(8,128)(4,1)S(1)} %fusion.148), kind=kLoop, calls=%fused_computation.17.clone.1 | loop fusion | flops 50331648 | bytes 84475904 | tf_op jit(solution)/shard_map/while/body/eval_jaxpr/convert_element_type | solution.py:96
  977.9 18.1 %bitcast_add_fusion.5 = f32[1024,16,64]{0,2,1:T(8,128)} fusion(f32[1024,16,64]{0,2,1:T(8,128)} %get-tuple-element.538, f32[16,512,1024]{2,1,0:T(8,128)} %fusion.147, f32[16,512]{1,0:T(8,128)S(1)} %dynamic-slice_bitcast_fusion.2, pred[512,1024]{1,0:T(8,128)(4,1)S(1)} %fusion.148, pred[]{:T(512)S(6)} %compare.4, ...), kind=kOutput, calls=%fused_computation.23.clone.1 | convolution fusion | flops 1109393408 | bytes 43548676 | tf_op jit(solution)/shard_map/while/body/eval_jaxpr/hqk,qhd->khd/dot_general | solution.py:89
  998.5 17.1 %fusion.147 = f32[16,512,1024]{2,1,0:T(8,128)} fusion(bf16[1024,16,64]{0,2,1:T(8,128)(2,1)S(1)} %get-tuple-element.557, bf16[1024,16,64]{0,2,1:T(8,128)(2,1)} %get-tuple-element.555, s32[]{:T(128)S(6)} %select_n.90), kind=kOutput, calls=%fused_computation.32.clone.1 | convolution fusion | flops 1073741824 | bytes 36700164 | tf_op jit(solution)/shard_map/while/body/eval_jaxpr/qhd,khd->hqk/dot_general | solution.py:53
  1017.4 25.7 %multiply_reduce_fusion.13 = (f32[16,512]{1,0:T(8,128)S(1)}, f32[16,512,1024]{2,1,0:T(8,128)}) fusion(f32[16,512,1024]{2,1,0:T(8,128)} %fusion.147, f32[16,512]{1,0:T(8,128)S(1)} %dynamic-slice_bitcast_fusion.2, pred[512,1024]{1,0:T(8,128)(4,1)S(1)} %fusion.148, bf16[1024,16,64]{0,2,1:T(8,128)(2,1)S(1)} %copy-done.8, ...), kind=kOutput, calls=%fused_computation.18.clone.1 | convolution fusion | flops 1115676672 | bytes 70844416 | tf_op jit(solution)/shard_map/while/body/eval_jaxpr/qhd,khd->hqk/dot_general | solution.py:86
  1043.1 28.1 %multiply_convert_fusion.6 = bf16[16,512,1024]{2,1,0:T(8,128)(2,1)} fusion(f32[16,512,1024]{2,1,0:T(8,128)} %get-tuple-element.487, f32[16,512,1024]{2,1,0:T(8,128)} %fusion.147, f32[16,512]{1,0:T(8,128)S(1)} %get-tuple-element.488, f32[16,512]{1,0:T(8,128)S(1)} %dynamic-slice_bitcast_fusion.2, pred[512,1024]{1,0:T(8,128)(4,1)S(1)} %fusion.148), kind=kLoop, calls=%fused_computation.17.clone.1 | loop fusion | flops 50331648 | bytes 84475904 | tf_op jit(solution)/shard_map/while/body/eval_jaxpr/convert_element_type | solution.py:96
  1092.6 19.2 %bitcast_add_fusion.5 = f32[1024,16,64]{0,2,1:T(8,128)} fusion(f32[1024,16,64]{0,2,1:T(8,128)} %get-tuple-element.538, f32[16,512,1024]{2,1,0:T(8,128)} %fusion.147, f32[16,512]{1,0:T(8,128)S(1)} %dynamic-slice_bitcast_fusion.2, pred[512,1024]{1,0:T(8,128)(4,1)S(1)} %fusion.148, pred[]{:T(512)S(6)} %compare.4, ...), kind=kOutput, calls=%fused_computation.23.clone.1 | convolution fusion | flops 1109393408 | bytes 43548676 | tf_op jit(solution)/shard_map/while/body/eval_jaxpr/hqk,qhd->khd/dot_general | solution.py:89
  1184.2 39.8 %all-reduce = (f32[1024]{0:T(1024)}, f32[1024]{0:T(1024)}, f32[1024]{0:T(1024)}, f32[1024]{0:T(1024)}, f32[16]{0:T(128)}, /*index=5*/f32[1024]{0:T(1024)}, f32[1...) all-reduce(f32[1024]{0:T(1024)S(1)} %get-tuple-element.263, ...), channel_id=1, replica_groups=mesh['rows'=4,'ffn'=8] {'rows','ffn'}, use_global_device_ids=true, to_apply=%region_24.25 | all-reduce | flops 10256 | bytes 82048 | tf_op jit(solution)/shard_map/psum | solution.py:255
  1240.0 22.9 %reduce-scatter.12.cloned.1.call-done = f32[32,1024]{1,0:T(8,128)} async-done(((f32[1024,1024]{1,0:T(8,128)}), f32[32,1024]{1,0:T(8,128)}) %reduce-scatter.12.cloned.1.call-update) | async-done | bytes 131088 | tf_op jit(solution)/shard_map/reduce_scatter | solution.py:250
  1262.9 142.4 %reduce-scatter.16.cloned.1.call-done = f32[32,1024]{1,0:T(8,128)} async-done(((f32[1024,1024]{1,0:T(8,128)}), f32[32,1024]{1,0:T(8,128)}) %reduce-scatter.16.cloned.1.call-update) | async-done | bytes 131088 | tf_op jit(solution)/shard_map/reduce_scatter | solution.py:252
  1405.3 142.4 %reduce-scatter.14.cloned.1.call-done = f32[32,1024]{1,0:T(8,128)} async-done(((f32[1024,1024]{1,0:T(8,128)}), f32[32,1024]{1,0:T(8,128)}) %reduce-scatter.14.cloned.1.call-update) | async-done | bytes 131088 | tf_op jit(solution)/shard_map/reduce_scatter | solution.py:251
  (352 shorter events, 451.4 us)
Async XLA Ops:
  7.2 32.0 %all-gather.14.cloned.1.call-start = ((), (), s32[]{:S(2)}) async-start(), calls=%async_computation.12 | async-start | bytes 1310720 | tf_op jit(solution)/shard_map/all_gather | solution.py:174
  7.9 87.7 %all-gather.18.cloned.1.call-start = ((), (), s32[]{:S(2)}) async-start(), calls=%async_computation.14 | async-start | bytes 1310720 | tf_op jit(solution)/shard_map/all_gather | solution.py:175
  8.7 124.7 %all-gather.10.cloned.1.call-start = ((), (), s32[]{:S(2)}) async-start(), calls=%async_computation.10 | async-start | bytes 2162688 | tf_op jit(solution)/shard_map/all_gather | solution.py:152
  9.4 182.2 %all-gather.8.cloned.1.call-start = ((), (), s32[]{:S(2)}) async-start(), calls=%async_computation.9 | async-start | bytes 2162688 | tf_op jit(solution)/shard_map/all_gather | solution.py:150
  10.0 383.6 %all-gather.12.cloned.1.call-start = ((), (), s32[]{:S(2)}) async-start(), calls=%async_computation.11 | async-start | bytes 2162688 | tf_op jit(solution)/shard_map/all_gather | solution.py:153
  10.6 397.5 %all-gather.16.cloned.1.call-start = ((), (), s32[]{:S(2)}) async-start(), calls=%async_computation.13 | async-start | bytes 9437184 | tf_op jit(solution)/shard_map/all_gather | solution.py:178
  39.3 420.0 %all-gather.20.cloned.1.call-start = ((), (), s32[]{:S(2)}) async-start(), calls=%async_computation.15 | async-start | bytes 9437184 | tf_op jit(solution)/shard_map/all_gather | solution.py:179
  39.3 5.9 collective-permute-start
  46.1 5.0 collective-permute-start.1
  52.0 15.1 collective-permute-start.2
  68.0 14.0 collective-permute-start.3
  83.1 26.0 %collective-permute-start.4 = (bf16[512,1024]{1,0:T(8,128)(2,1)}, bf16[512,1024]{1,0:T(8,128)(2,1)S(1)}, u32[]{:S(2)}, u32[]{:S(2)}) collective-permute-start(bf16[512,1024]{1,0:T(8,128)(2,1)} %get-tuple-element.339), channel_id=1, source_target_pairs={{0,16},{1,17},{2,18},{3,19},{4,20},{5,21},{6,22},{7,23},{8,24},{9,... | collective-permute-start | bytes 3145736 | tf_op jit(solution)/shard_map/ppermute | solution.py:15
  94.4 97.2 %copy-start.38 = (f32[1024]{0:T(1024)}, f32[1024]{0:T(1024)S(1)}, u32[]{:S(2)}) copy-start(f32[1024]{0:T(1024)S(1)} %broadcast_multiply_fusion.5) | copy-start | bytes 12292
  95.6 96.0 %copy-start.44 = (f32[1024]{0:T(1024)}, f32[1024]{0:T(1024)S(1)}, u32[]{:S(2)}) copy-start(f32[1024]{0:T(1024)S(1)} %fusion.54) | copy-start | bytes 12292
  95.7 599.2 %reduce-scatter.20.cloned.1.call-start = ((), (), s32[]{:S(2)}) async-start(), calls=%async_computation.20 | async-start | bytes 18874368 | tf_op jit(solution)/shard_map/reduce_scatter | solution.py:209
  122.0 69.6 %copy-start.77 = (f32[1024]{0:T(1024)S(1)}, f32[1024]{0:T(1024)}, u32[]{:S(2)}) copy-start(f32[1024]{0:T(1024)} %param.33) | copy-start | bytes 12292
  527.5 336.3 %reduce-scatter.24.cloned.1.call-start = ((), (), s32[]{:S(2)}) async-start(), calls=%async_computation.22 | async-start | bytes 18874368 | tf_op jit(solution)/shard_map/reduce_scatter | solution.py:210
  542.0 682.0 %reduce-scatter.28.cloned.1.call-start = ((), (), s32[]{:S(2)}) async-start(), calls=%async_computation.24 | async-start | bytes 2359296
  569.6 666.8 %reduce-scatter.22.cloned.1.call-start = ((), (), s32[]{:S(2)}) async-start(), calls=%async_computation.21 | async-start | bytes 1310720 | tf_op jit(solution)/shard_map/reduce_scatter | solution.py:214
  697.6 540.6 %reduce-scatter.26.cloned.1.call-start = ((), (), s32[]{:S(2)}) async-start(), calls=%async_computation.23 | async-start | bytes 1310720 | tf_op jit(solution)/shard_map/reduce_scatter | solution.py:217
  866.5 373.5 %reduce-scatter.18.cloned.1.call-start = ((), (), s32[]{:S(2)}) async-start(), calls=%async_computation.19 | async-start | bytes 4325376 | tf_op jit(solution)/shard_map/reduce_scatter | solution.py:253
  880.2 382.7 %reduce-scatter.12.cloned.1.call-start = ((), (), s32[]{:S(2)}) async-start(), calls=%async_computation.16 | async-start | bytes 4325376 | tf_op jit(solution)/shard_map/reduce_scatter | solution.py:250
  1122.2 283.1 %reduce-scatter.16.cloned.1.call-start = ((), (), s32[]{:S(2)}) async-start(), calls=%async_computation.18 | async-start | bytes 4325376 | tf_op jit(solution)/shard_map/reduce_scatter | solution.py:252
  1130.5 417.1 %reduce-scatter.14.cloned.1.call-start = ((), (), s32[]{:S(2)}) async-start(), calls=%async_computation.17 | async-start | bytes 4325376 | tf_op jit(solution)/shard_map/reduce_scatter | solution.py:251
  (85 other events, 941.2 us)
Sparse Core Ops, SparseCore 0:
  9.9 29.3 all-gather.13
  41.1 28.0 all-gather.17
  72.1 61.2 all-gather.9
  136.2 55.3 all-gather.7
  194.4 55.3 all-gather.11
  251.3 80.9 all-gather.15
  333.8 80.6 all-gather.19
  527.7 167.1 reduce-scatter.19
  697.2 166.5 reduce-scatter.23
  866.0 34.2 reduce-scatter.27
  903.1 26.1 reduce-scatter.21
  932.3 27.7 reduce-scatter.25
  962.9 142.5 reduce-scatter.17
  1122.3 140.5 reduce-scatter.11
  1265.6 139.6 reduce-scatter.15
  1408.0 139.6 reduce-scatter.13
